TPU v7x, 256 devices: a whole 4x4x8 slice. The times are simulated.
256 devices in a mesh: row: 16 (over x, z_lo), col: 16 (over z_hi, y, core).
Axes of the slice: x: 4, y: 4, z: 8 (z_hi: 2, z_lo: 4; z = z_hi * 4 + z_lo), core: 2. Of those that a mesh axis runs over, the one named last changes fastest.
Arguments:
- factors: bfloat16 [32768, 256], P(('row', 'col')), may hold values from -1.5 to 1.5
- cores: bfloat16 [8, 256, 256], replicated, may hold values from -0.375 to 0.375
- tiles: bfloat16 [8192, 256, 256], P(('row', 'col')), may hold values from -6 to 6
- tile_coords: int32 [8192, 3], P(('row', 'col')), may hold values from 0 to 7, as said below
- tile_counts: int32 [256], P(('row', 'col')), may hold values from 1 to 32, as said below
Outputs:
- gradient: float32 [32768, 256], P(('row', 'col'))
Inputs may be any that keep to these rules, and one draw needn't show every extreme that they name: `tile_coords`: column 0 is a relation below 8, column 1 below 8, column 2 below 8; within one device no two slots have the same three coordinates. `tile_counts`: some device has all 32 slots live.
All inputs are finite; a program needn't handle non-finite values.
Results may differ from a plain program's by a relative error of at most 0.0011.
Values may be sent and summed in bfloat16 or wider, within the bound.
A program may use at most 128 MiB of HBM per device.

v0:
```python
import jax
import jax.numpy as jnp
from jax import lax
from jax.sharding import PartitionSpec as P

weight_decay = 1.0


def broadcast(value, axis, source):
    kept = jnp.where(lax.axis_index(axis) == source, value, 0).astype(value.dtype)
    return lax.psum(kept, axis)


def local(factors, cores, tiles, tile_coords, tile_counts):
    n_row = lax.axis_size("row")
    n_col = lax.axis_size("col")
    row_ratio = n_row // n_col
    shard_rows, rank_width = factors.shape
    tile_size = tiles.shape[1]
    relations = cores.shape[0]
    src_rows = shard_rows * n_col
    tgt_rows = src_rows * row_ratio
    src_blocks = src_rows // tile_size
    tgt_blocks = tgt_rows // tile_size
    row_pos = lax.axis_index("row")
    col_pos = lax.axis_index("col")
    source = lax.all_gather(factors, "col", axis=0, tiled=True)
    received = broadcast(source, "row", col_pos * row_ratio + 0)
    left_core = jnp.einsum("nr,krs->kns", source, cores, preferred_element_type=jnp.float32).astype(
        jnp.bfloat16
    )
    left_core = left_core.reshape(relations, src_blocks, tile_size, rank_width)
    right_core = jnp.einsum(
        "nr,ksr->kns", received, cores, preferred_element_type=jnp.float32
    ).astype(jnp.bfloat16)
    right_core = right_core.reshape(relations, tgt_blocks, tile_size, rank_width)
    tgt_factor = received.reshape(tgt_blocks, tile_size, rank_width)
    live_count = tile_counts[0]

    def group_pass(group, carry):
        grad_src, grad_tgt = carry
        start = group * 8
        coords = lax.dynamic_slice_in_dim(tile_coords, start, 8, 0)
        values = lax.dynamic_slice_in_dim(tiles, start, 8, 0)
        is_live = start + jnp.arange(8, dtype=jnp.int32) < live_count
        relation = coords[:, 0]
        src_index = coords[:, 1]
        tgt_index = coords[:, 2]
        left = left_core[relation, src_index]
        right = tgt_factor[tgt_index]
        right_rel = right_core[relation, tgt_index]
        predicted = jnp.einsum("gtr,gur->gtu", left, right, preferred_element_type=jnp.float32)
        resid = jnp.where(
            is_live[:, None, None], values.astype(jnp.float32) - predicted, 0.0
        ).astype(jnp.bfloat16)
        src_grad = jnp.einsum("gtu,gur->gtr", resid, right_rel, preferred_element_type=jnp.float32)
        tgt_grad = jnp.einsum("gtu,gtr->gur", resid, left, preferred_element_type=jnp.float32)
        return (grad_src.at[src_index].add(src_grad), grad_tgt.at[tgt_index].add(tgt_grad))

    start_grads = (
        jnp.zeros((src_blocks, tile_size, rank_width), jnp.float32),
        jnp.zeros((tgt_blocks, tile_size, rank_width), jnp.float32),
    )
    grad_src, grad_tgt = lax.fori_loop(0, (live_count + 7) // 8, group_pass, start_grads)
    grad_src = grad_src.reshape(src_rows, rank_width)
    grad_tgt = grad_tgt.reshape(tgt_rows, rank_width)
    tgt_total = lax.psum(grad_tgt, "row")
    summed = lax.psum_scatter(grad_src, "col", scatter_dimension=0, tiled=True)
    relay_block = broadcast(tgt_total, "col", row_pos // row_ratio)
    relay_part = lax.dynamic_slice_in_dim(
        relay_block, (row_pos % row_ratio * n_col + col_pos) * shard_rows, shard_rows, 0
    )
    summed = summed + relay_part
    return weight_decay * factors.astype(jnp.float32) - summed / tile_size


def solution(mesh):
    in_specs = (
        P(("row", "col"), None),
        P(),
        P(("row", "col"), None, None),
        P(("row", "col"), None),
        P(("row", "col")),
    )
    out_specs = P(("row", "col"), None)
    return jax.shard_map(local, mesh=mesh, in_specs=in_specs, out_specs=out_specs, check_vma=False)
```

profile of v0, /device:TPU:1, one launch (start us, length us, event | category | flops | bytes accessed | tf_op | source)
XLA Modules:
  0.0 805.9 jit_solution(2866157427274746892)
XLA Ops:
  6.5 0.0 copy-start
  6.5 0.0 all-gather.2.cloned.1.call-start
  6.5 0.7 all-gather.2.cloned.1.call-update
  7.3 0.0 all-reduce.4.cloned.1.call-start
  7.3 62.5 %all-gather.2.cloned.1.call-done = bf16[2048,256]{1,0:T(8,128)(2,1)} async-done(((bf16[128,256]{1,0:T(8,128)(2,1)}), bf16[2048,256]{1,0:T(8,128)(2,1)}) %all-gather.2.cloned.1.call-update) | async-done | bytes 1048592 | tf_op jit(solution)/shard_map/all_gather | solution.py:27
  69.8 1.1 broadcast_select_fusion.1
  70.9 0.0 all-reduce.4.cloned.1.call-update
  70.9 0.0 all-reduce.6.cloned.1.call-start
  71.6 0.0 copy-done
  71.6 0.0 copy-done.3
  71.7 5.6 convert_bitcast_fusion
  77.3 11.4 %copy.11 = bf16[8,2048,256]{2,1,0:T(8,128)(2,1)} copy(bf16[8,2048,256]{1,2,0:T(8,128)(2,1)} %convert_bitcast_fusion) | data formatting | bytes 16777216 | tf_op jit(solution)/shard_map/while | solution.py:64
  88.7 135.2 %all-reduce.4.cloned.1.call-done = bf16[2048,256]{1,0:T(8,128)(2,1)} async-done(((bf16[2048,256]{1,0:T(8,128)(2,1)}), bf16[2048,256]{1,0:T(8,128)(2,1)}) %all-reduce.4.cloned.1.call-update) | async-done | bytes 1048592 | tf_op jit(solution)/shard_map/psum | solution.py:11
  223.9 6.8 convolution_convert_fusion
  230.7 1.5 broadcast.27.clone
  232.1 1.5 broadcast.27
  233.7 82.3 %while.12 = (s32[]{:T(128)}, f32[8,256,256]{2,1,0:T(8,128)}, f32[8,256,256]{2,1,0:T(8,128)}, s32[]{:T(128)}, s32[32,3]{0,1:T(4,128)S(1)}, /*index=5*/s32[]{:T(12...) while((s32[]{:T(128)}, f32[8,256,256]{2,1,0:T(8,128)}, ...), condition=%wide.region_4.5_spmd, body=%wide.region_1.4_spmd.sunk | while | flops 808453248 | bytes 39850920 | solution.py:64
  233.7 0.7 add_compare_fusion.2
  234.3 0.1 constant_dynamic-slice_fusion.2
  234.4 1.8 gather_fusion.1
  236.3 4.0 gather_fusion
  240.3 1.0 copy-done.1
  241.3 1.7 select_convert_fusion.2
  243.0 1.0 copy-done.2
  244.0 1.7 fusion.31
  245.7 4.1 scatter_fusion.1
  249.9 5.0 gather_fusion.2
  254.8 2.0 fusion.30
  256.8 4.2 scatter_fusion
  261.1 0.7 add_compare_fusion.2
  261.7 0.1 constant_dynamic-slice_fusion.2
  261.8 1.8 gather_fusion.1
  263.7 4.0 gather_fusion
  267.7 1.0 copy-done.1
  268.7 1.7 select_convert_fusion.2
  270.4 0.0 copy-start.2
  270.4 1.0 copy-done.2
  271.4 1.7 fusion.31
  273.1 4.2 scatter_fusion.1
  277.3 5.0 gather_fusion.2
  282.3 2.0 fusion.30
  284.3 4.3 scatter_fusion
  288.6 0.7 add_compare_fusion.2
  289.2 0.1 constant_dynamic-slice_fusion.2
  289.3 1.8 gather_fusion.1
  291.2 4.0 gather_fusion
  295.2 1.0 copy-done.1
  296.2 1.7 select_convert_fusion.2
  297.9 1.0 copy-done.2
  298.9 1.7 fusion.31
  300.6 4.2 scatter_fusion.1
  304.8 5.0 gather_fusion.2
  309.8 2.0 fusion.30
  311.7 4.2 scatter_fusion
  315.9 0.0 all-reduce.6.cloned.1.call-update
  316.0 0.0 reduce-scatter.2.cloned.1.call-start
  316.0 0.5 reduce-scatter.2.cloned.1.call-update
  316.5 0.0 all-reduce.8.cloned.1.call-start
  316.6 199.1 %all-reduce.6.cloned.1.call-done = f32[2048,256]{1,0:T(8,128)} async-done(((f32[2048,256]{1,0:T(8,128)}), f32[2048,256]{1,0:T(8,128)}) %all-reduce.6.cloned.1.call-update) | async-done | bytes 2097168 | tf_op jit(solution)/shard_map/psum | solution.py:67
  515.7 1.4 broadcast_select_fusion
  517.2 0.0 all-reduce.8.cloned.1.call-update
  517.2 95.2 %reduce-scatter.2.cloned.1.call-done = f32[128,256]{1,0:T(8,128)} async-done(((f32[2048,256]{1,0:T(8,128)}), f32[128,256]{1,0:T(8,128)}) %reduce-scatter.2.cloned.1.call-update) | async-done | bytes 131088 | tf_op jit(solution)/shard_map/reduce_scatter | solution.py:68
  612.4 185.3 %all-reduce.8.cloned.1.call-done = f32[2048,256]{1,0:T(8,128)} async-done(((f32[2048,256]{1,0:T(8,128)}), f32[2048,256]{1,0:T(8,128)}) %all-reduce.8.cloned.1.call-update) | async-done | bytes 2097168 | tf_op jit(solution)/shard_map/psum | solution.py:11
  797.7 1.6 multiply_subtract_fusion
  (16 shorter events, 0.1 us)
Async XLA Ops:
  6.5 65.1 %copy-start = (bf16[8,256,256]{2,1,0:T(8,128)(2,1)S(1)}, bf16[8,256,256]{2,1,0:T(8,128)(2,1)}, u32[]{:S(2)}) copy-start(bf16[8,256,256]{2,1,0:T(8,128)(2,1)} %param.8) | copy-start | bytes 3145732
  6.5 63.3 %all-gather.2.cloned.1.call-start = ((), (), s32[]{:S(2)}) async-start(), calls=%async_computation.1 | async-start | bytes 1114112 | tf_op jit(solution)/shard_map/all_gather | solution.py:27
  7.3 216.6 %all-reduce.4.cloned.1.call-start = ((), (), s32[]{:S(2)}) async-start(), calls=%async_computation.2 | async-start | bytes 2097152 | tf_op jit(solution)/shard_map/psum | solution.py:11
  69.8 1.8 copy-start.3
  70.9 444.8 %all-reduce.6.cloned.1.call-start = ((), (), s32[]{:S(2)}) async-start(), calls=%async_computation.4 | async-start | bytes 4194304 | tf_op jit(solution)/shard_map/psum | solution.py:67
  230.7 3.0 copy-start.5
  240.3 1.0 copy-start.1
  243.0 1.0 copy-start.2
  267.7 1.0 copy-start.1
  270.4 1.0 copy-start.2
  295.2 1.0 copy-start.1
  297.9 1.0 copy-start.2
  316.0 296.5 %reduce-scatter.2.cloned.1.call-start = ((), (), s32[]{:S(2)}) async-start(), calls=%async_computation.3 | async-start | bytes 2228224 | tf_op jit(solution)/shard_map/reduce_scatter | solution.py:68
  316.5 481.2 %all-reduce.8.cloned.1.call-start = ((), (), s32[]{:S(2)}) async-start(), calls=%async_computation.5 | async-start | bytes 4194304 | tf_op jit(solution)/shard_map/psum | solution.py:11
  517.2 280.6 %copy-start.4 = (bf16[128,256]{1,0:T(8,128)(2,1)S(1)}, bf16[128,256]{1,0:T(8,128)(2,1)}, u32[]{:S(2)}) copy-start(bf16[128,256]{1,0:T(8,128)(2,1)} %param.7) | copy-start | bytes 196612
Sparse Core Ops, SparseCore 0:
  10.1 59.7 all-gather.1
  72.5 151.3 all-reduce.3
  316.1 199.6 all-reduce.5
  519.8 92.5 reduce-scatter.1
  614.9 182.7 all-reduce.7
where the time goes:
time: 807 us; the launch traced here: 806 us
  waiting for transfers between devices  679 us (84%)
  local copies, waits for them, and re-layouts  53 us (7%)
  other arithmetic  31.4 us (4%)
  matrix products  28.6 us (4%)
  between operations  13.8 us (2%)
    psum x2, waiting for transfers between devices, broadcast(): return lax.psum(kept, axis)  320 us
    psum x1, waiting for transfers between devices, local(): tgt_total = lax.psum(grad_tgt, 'row')  199 us
    reduce_scatter x1, waiting for transfers between devices, local(): summed = lax.psum_scatter(grad_src, 'col', scatter_dimension=0, tiled=True)  95.2 us
    all_gather x1, waiting for transfers between devices, local(): source = lax.all_gather(factors, 'col', axis=0, tiled=True)  62.5 us
  transfers between devices with their start and end apart: 5, of which 5 were waited for; matrix products, arithmetic and copies ran while one was open for 2% of the time, Pallas kernels for 0%

commit v1 on v0

--- a/solution.py
+++ b/solution.py
@@ -8,7 +8,7 @@
 
 def broadcast(value, axis, source):
     kept = jnp.where(lax.axis_index(axis) == source, value, 0).astype(value.dtype)
-    return lax.psum(kept, axis)
+    return jnp.sum(lax.all_gather(kept, axis_name=axis), axis=0)
 
 
 def local(factors, cores, tiles, tile_coords, tile_counts):

time: 807 us -> 1130 us (1.40)
  waiting for transfers between devices: 679 us -> 978 us
  other arithmetic: 31.4 us -> 53.5 us
    all_gather x0 -> x2, waiting for transfers between devices: none -> 650 us  [broadcast(): return jnp.sum(lax.all_gather(kept, axis_name=axis), axis=0)]
    psum x2 -> x0, waiting for transfers between devices: 320 us -> none  [broadcast(): return lax.psum(kept, axis)]
    reduce_scatter x1, waiting for transfers between devices: 95.2 us -> 71.4 us  [local(): summed = lax.psum_scatter(grad_src, 'col', scatter_dimension=0, tiled=True)]
    reduce_sum x0 -> x2, other arithmetic: none -> 22.2 us  [broadcast(): return jnp.sum(lax.all_gather(kept, axis_name=axis), axis=0)]
  transfers between devices with their start and end apart: 5 -> 5, of which waited for: 5 -> 5; matrix products, arithmetic and copies ran while one was open for 2% -> 3% of each run, Pallas kernels for 0% -> 0%
where the time goes in v1:
time: 1130 us; the launch traced here: 1120 us
  waiting for transfers between devices  978 us (87%)
  other arithmetic  53.5 us (5%)
  local copies, waits for them, and re-layouts  47.1 us (4%)
  matrix products  31.6 us (3%)
  between operations  13.9 us (1%)
    all_gather x2, waiting for transfers between devices, broadcast(): return jnp.sum(lax.all_gather(kept, axis_name=axis), axis=0)  650 us
    psum x1, waiting for transfers between devices, local(): tgt_total = lax.psum(grad_tgt, 'row')  193 us
    reduce_scatter x1, waiting for transfers between devices, local(): summed = lax.psum_scatter(grad_src, 'col', scatter_dimension=0, tiled=True)  71.4 us
    all_gather x1, waiting for transfers between devices, local(): source = lax.all_gather(factors, 'col', axis=0, tiled=True)  62.5 us
  transfers between devices with their start and end apart: 5, of which 5 were waited for; matrix products, arithmetic and copies ran while one was open for 3% of the time, Pallas kernels for 0%

profile of v1, /device:TPU:1, one launch (start us, length us, event | category | flops | bytes accessed | tf_op | source)
XLA Modules:
  0.0 1123.9 jit_solution(10669330868088825802)
XLA Ops:
  6.5 0.0 copy-start
  6.5 0.0 all-gather.6.cloned.1.call-start
  6.5 0.7 all-gather.6.cloned.1.call-update
  7.3 0.0 all-gather.8.cloned.1.call-start
  7.3 62.5 %all-gather.6.cloned.1.call-done = bf16[2048,256]{1,0:T(8,128)(2,1)} async-done(((bf16[128,256]{1,0:T(8,128)(2,1)}), bf16[2048,256]{1,0:T(8,128)(2,1)}) %all-gather.6.cloned.1.call-update) | async-done | bytes 1048592 | tf_op jit(solution)/shard_map/all_gather | solution.py:27
  69.8 0.0 copy-start.2
  69.8 1.0 broadcast_select_fusion.1
  70.9 0.0 all-gather.8.cloned.1.call-update
  70.9 0.0 all-reduce.2.cloned.1.call-start
  71.6 0.0 copy-done
  71.6 0.0 copy-done.2
  71.7 5.6 convert_bitcast_fusion
  77.3 11.4 %copy.11 = bf16[8,2048,256]{2,1,0:T(8,128)(2,1)} copy(bf16[8,2048,256]{1,2,0:T(8,128)(2,1)} %convert_bitcast_fusion) | data formatting | bytes 16777216 | tf_op jit(solution)/shard_map/while | solution.py:64
  88.7 333.1 %all-gather.8.cloned.1.call-done = bf16[32768,256]{1,0:T(8,128)(2,1)} async-done(((bf16[2048,256]{1,0:T(8,128)(2,1)}), bf16[32768,256]{1,0:T(8,128)(2,1)}) %all-gather.8.cloned.1.call-update) | async-done | bytes 16777232 | tf_op jit(solution)/shard_map/all_gather | solution.py:11
  421.8 9.9 reduce_sum.21
  431.7 6.8 convolution_convert_fusion
  438.5 1.5 broadcast.27
  440.0 1.5 broadcast.27.clone
  441.5 0.0 copy-done.4
  441.5 79.0 %while.12 = (s32[]{:T(128)}, f32[8,256,256]{2,1,0:T(8,128)}, f32[8,256,256]{2,1,0:T(8,128)}, s32[]{:T(128)}, s32[32,3]{0,1:T(4,128)S(1)}, /*index=5*/s32[]{:T(12...) while((s32[]{:T(128)}, f32[8,256,256]{2,1,0:T(8,128)}, ...), condition=%wide.region_4.5_spmd, body=%wide.region_1.4_spmd.sunk | while | flops 808453248 | bytes 31462268 | solution.py:64
  441.5 0.1 constant_dynamic-slice_fusion.2
  441.6 4.0 gather_fusion
  445.6 1.8 gather_fusion.1
  447.5 0.7 add_compare_fusion.2
  448.2 2.7 select_convert_fusion.2
  450.8 5.0 gather_fusion.2
  455.8 2.0 fusion.30
  457.8 4.2 scatter_fusion
  462.0 1.7 fusion.31
  463.8 4.3 scatter_fusion.1
  468.0 0.1 constant_dynamic-slice_fusion.2
  468.1 4.0 gather_fusion
  472.1 1.8 gather_fusion.1
  474.0 0.7 add_compare_fusion.2
  474.6 2.7 select_convert_fusion.2
  477.3 5.0 gather_fusion.2
  482.3 2.0 fusion.30
  484.3 4.1 scatter_fusion
  488.4 1.7 fusion.31
  490.1 4.2 scatter_fusion.1
  494.4 0.1 constant_dynamic-slice_fusion.2
  494.5 4.0 gather_fusion
  498.5 1.8 gather_fusion.1
  500.3 0.7 add_compare_fusion.2
  501.0 2.7 select_convert_fusion.2
  503.7 5.0 gather_fusion.2
  508.6 2.0 fusion.30
  510.6 4.1 scatter_fusion
  514.7 1.7 fusion.31
  516.5 4.1 scatter_fusion.1
  520.6 0.0 all-reduce.2.cloned.1.call-update
  520.6 0.0 all-gather.10.cloned.1.call-start
  520.7 192.7 %all-reduce.2.cloned.1.call-done = f32[2048,256]{1,0:T(8,128)} async-done(((f32[2048,256]{1,0:T(8,128)}), f32[2048,256]{1,0:T(8,128)}) %all-reduce.2.cloned.1.call-update) | async-done | bytes 2097168 | tf_op jit(solution)/shard_map/psum | solution.py:67
  713.4 1.5 broadcast_select_fusion
  714.9 0.0 all-gather.10.cloned.1.call-update
  714.9 0.0 reduce-scatter.2.cloned.1.call-start
  715.0 0.5 reduce-scatter.2.cloned.1.call-update
  715.5 316.6 %all-gather.10.cloned.1.call-done = f32[32768,256]{1,0:T(8,128)} async-done(((f32[2048,256]{1,0:T(8,128)}), f32[32768,256]{1,0:T(8,128)}) %all-gather.10.cloned.1.call-update) | async-done | bytes 33554448 | tf_op jit(solution)/shard_map/all_gather | solution.py:11
  1032.2 0.0 copy-start.1
  1032.2 12.3 %reduce_sum.22 = f32[2048,256]{1,0:T(8,128)S(1)} reduce(f32[16,2048,256]{2,1,0:T(8,128)} %bitcast.51, f32[]{:T(128)} %constant.59.clone.1), dimensions={0}, to_apply=%region_7.8 | reduce | flops 7864320 | bytes 35651588 | tf_op jit(solution)/shard_map/reduce_sum | solution.py:11
  1044.4 71.4 %reduce-scatter.2.cloned.1.call-done = f32[128,256]{1,0:T(8,128)} async-done(((f32[2048,256]{1,0:T(8,128)}), f32[128,256]{1,0:T(8,128)}) %reduce-scatter.2.cloned.1.call-update) | async-done | bytes 131088 | tf_op jit(solution)/shard_map/reduce_scatter | solution.py:68
  1115.8 0.0 copy-done.3
  1115.8 1.6 multiply_subtract_fusion
  1117.4 0.0 copy-done.1
  (8 shorter events, 0.1 us)
Async XLA Ops:
  6.5 65.1 %copy-start = (bf16[8,256,256]{2,1,0:T(8,128)(2,1)S(1)}, bf16[8,256,256]{2,1,0:T(8,128)(2,1)}, u32[]{:S(2)}) copy-start(bf16[8,256,256]{2,1,0:T(8,128)(2,1)} %param.8) | copy-start | bytes 3145732
  6.5 63.3 %all-gather.6.cloned.1.call-start = ((), (), s32[]{:S(2)}) async-start(), calls=%async_computation.1 | async-start | bytes 1114112 | tf_op jit(solution)/shard_map/all_gather | solution.py:27
  7.3 414.5 %all-gather.8.cloned.1.call-start = ((), (), s32[]{:S(2)}) async-start(), calls=%async_computation.4 | async-start | bytes 17825792 | tf_op jit(solution)/shard_map/all_gather | solution.py:11
  69.8 1.8 copy-start.2
  70.9 642.5 %all-reduce.2.cloned.1.call-start = ((), (), s32[]{:S(2)}) async-start(), calls=%async_computation.3 | async-start | bytes 4194304 | tf_op jit(solution)/shard_map/psum | solution.py:67
  438.5 3.0 copy-start.4
  520.6 511.6 %all-gather.10.cloned.1.call-start = ((), (), s32[]{:S(2)}) async-start(), calls=%async_computation.5 | async-start | bytes 35651584 | tf_op jit(solution)/shard_map/all_gather | solution.py:11
  714.9 400.9 %reduce-scatter.2.cloned.1.call-start = ((), (), s32[]{:S(2)}) async-start(), calls=%async_computation.2 | async-start | bytes 2228224 | tf_op jit(solution)/shard_map/reduce_scatter | solution.py:68
  1032.2 83.6 %copy-start.3 = (bf16[128,256]{1,0:T(8,128)(2,1)S(1)}, bf16[128,256]{1,0:T(8,128)(2,1)}, u32[]{:S(2)}) copy-start(bf16[128,256]{1,0:T(8,128)(2,1)} %param.7) | copy-start | bytes 196612
  1032.2 85.2 %copy-start.1 = (bf16[8,256,256]{2,1,0:T(8,128)(2,1)S(1)}, bf16[8,256,256]{2,1,0:T(8,128)(2,1)}, u32[]{:S(2)}) copy-start(bf16[8,256,256]{2,1,0:T(8,128)(2,1)} %param.8) | copy-start | bytes 3145732
Sparse Core Ops, SparseCore 0:
  10.1 59.7 all-gather.5
  71.6 350.0 all-gather.7
  520.7 192.6 all-reduce.1
  716.0 316.1 all-gather.9
  1036.3 79.5 reduce-scatter.1
